TPU v7x, 32 devices: a whole 2x2x4 slice. The times are simulated.
32 devices in a mesh: group: 4 (over z), shard: 8 (over y, x, core).
Axes of the slice: x: 2, y: 2, z: 4, core: 2. Of those that a mesh axis runs over, the one named last changes fastest.
Arguments:
- query_hidden: bfloat16 [32, 32, 768], P(('group', 'shard')), may hold values from -6 to 6
- positive_hidden: bfloat16 [32, 64, 768], P(('group', 'shard')), may hold values from -6 to 6
- passage_store: bfloat16 [256, 64, 768], P('shard'), may hold values from -6 to 6
- negative_ids: int32 [32, 8], P(('group', 'shard')), may hold values from 0 to 255, as said below
- teacher_margins: int32 [32, 8], P(('group', 'shard')), may hold values from -4096 to 4095
- transform_weight: bfloat16 [768, 768], replicated, may hold values from -0.21875 to 0.21875
- vocab_weight: bfloat16 [768, 15360], P(None, 'shard'), may hold values from -0.21875 to 0.21875
- dense_weight: bfloat16 [768, 768], replicated, may hold values from -0.21875 to 0.21875
Outputs:
- student_margin: float32 [32, 8], P(('group', 'shard'))
- dense_grad: float32 [768, 768], replicated
Inputs may be any that keep to these rules, and one draw needn't show every extreme that they name: `negative_ids`: passage p is held by shard index p // 32. Among the 8 negatives of one index of group and shard, every store index is named by none or exactly 2 of them; one store index, drawn from the seed, is named 2 times by every index of group and shard.
All inputs are finite; a program needn't handle non-finite values.
Results may differ from a plain program's by a relative error of at most 0.0029.
Values may be sent and summed in bfloat16 or wider, within the bound.
A program may use at most 128 MiB of HBM per device.

v0:
```python
from functools import partial
import math
import jax
import jax.numpy as jnp
from jax import lax
from jax.sharding import PartitionSpec as P

CAP = 2


def encode(hidden, transform_weight):
    mixed_rows = jnp.dot(hidden, transform_weight, preferred_element_type=jnp.float32)
    active = jax.nn.gelu(mixed_rows, approximate=False)
    centre = jnp.mean(active, axis=-1, keepdims=True)
    spread = jnp.mean(jnp.square(active - centre), axis=-1, keepdims=True)
    return ((active - centre) * lax.rsqrt(spread + 1e-05)).astype(jnp.bfloat16)


def pool_single(sequence, vocab_weight):
    logits = jnp.dot(sequence, vocab_weight, preferred_element_type=jnp.float32)
    return jnp.max(jnp.log1p(jnp.maximum(logits, 0.0)), axis=0)


def pool_sequences(block_rows, offset, vocab_weight):
    return lax.map(partial(pool_single, vocab_weight=vocab_weight), block_rows, batch_size=8)


def add_outer(running, pieces):
    return running + jnp.einsum("rd,re->de", pieces[0], pieces[1], precision=lax.Precision.HIGHEST)


def body(
    query_hidden,
    positive_hidden,
    passage_store,
    negative_ids,
    teacher_margins,
    transform_weight,
    vocab_weight,
    dense_weight,
):
    shards = lax.axis_size("shard")
    queries_dev, negatives = negative_ids.shape
    store_rows, length, width = passage_store.shape
    vocab_total = vocab_weight.shape[1] * shards
    pooler = partial(pool_sequences, vocab_weight=vocab_weight)
    query_coded = encode(query_hidden, transform_weight)
    positive_coded = encode(positive_hidden, transform_weight)
    query_pool = pooler(lax.all_gather(query_coded, "shard", axis=0, tiled=True), jnp.int32(0))
    neg_total = queries_dev * negatives
    flat_ids = negative_ids.reshape(neg_total)
    owner_of = flat_ids // store_rows
    local_row = flat_ids % store_rows
    shard_ids = jnp.arange(shards, dtype=jnp.int32)
    owner_hit = (owner_of[:, None] == shard_ids[None, :]).astype(jnp.int32)
    earlier = jnp.cumsum(owner_hit, axis=0) - owner_hit
    slot_rank = jnp.sum(earlier * owner_hit, axis=1)
    slot_ids = jnp.arange(CAP, dtype=jnp.int32)
    slot_hit = (owner_hit[:, :, None] > 0) & (slot_rank[:, None, None] == slot_ids[None, None, :])
    asked_rows = jnp.sum(jnp.where(slot_hit, local_row[:, None, None], 0), axis=0)
    requests = jnp.where(jnp.any(slot_hit, axis=0), asked_rows, -1)
    asked_for = lax.all_to_all(requests, "shard", split_axis=0, concat_axis=0, tiled=True)
    is_valid = asked_for >= 0
    served = passage_store[jnp.clip(asked_for, 0, store_rows - 1)]
    served = jnp.where(is_valid[:, :, None, None], served, jnp.zeros((), served.dtype))
    fetched = lax.all_to_all(served, "shard", split_axis=0, concat_axis=0, tiled=True)
    negative_hidden = fetched.reshape(shards * CAP, length, width)[owner_of * CAP + slot_rank]
    negative_coded = encode(negative_hidden, transform_weight)
    passages = jnp.concatenate(
        [positive_coded[:, None], negative_coded.reshape(queries_dev, negatives, length, width)],
        axis=1,
    )
    passages = passages.reshape(queries_dev * (1 + negatives), length, width)
    passage_pool = pooler(lax.all_gather(passages, "shard", axis=0, tiled=True), jnp.int32(0))
    passage_pool = passage_pool.reshape(shards * queries_dev, 1 + negatives, -1)
    pair_terms = jnp.einsum("qv,qjv->qj", query_pool, passage_pool, precision=lax.Precision.HIGHEST)
    sparse = lax.psum_scatter(pair_terms, "shard", scatter_dimension=0, tiled=True) / math.sqrt(
        vocab_total
    )
    inv_root = 1.0 / math.sqrt(width)
    query_cls = query_hidden[:, 0, :]
    positive_cls = positive_hidden[:, 0, :]
    negative_cls = negative_hidden[:, 0, :].reshape(queries_dev, negatives, width)
    query_vec = jnp.dot(query_cls, dense_weight, preferred_element_type=jnp.float32)
    positive_vec = jnp.dot(positive_cls, dense_weight, preferred_element_type=jnp.float32)
    negative_vec = jnp.dot(negative_cls, dense_weight, preferred_element_type=jnp.float32)
    dense_pos = jnp.sum(query_vec * positive_vec, axis=1) * inv_root
    dense_neg = (
        jnp.einsum("qd,qkd->qk", query_vec, negative_vec, precision=lax.Precision.HIGHEST)
        * inv_root
    )
    pos_score = sparse[:, 0] + dense_pos
    neg_score = sparse[:, 1:] + dense_neg
    margin = pos_score[:, None] - neg_score
    target = teacher_margins.astype(jnp.float32) / 1024.0
    coef = (margin - target) / negatives
    coef_total = jnp.sum(coef, axis=1)
    grad_query = (
        coef_total[:, None] * positive_vec
        - jnp.einsum("qk,qkd->qd", coef, negative_vec, precision=lax.Precision.HIGHEST)
    ) * inv_root
    grad_positive = coef_total[:, None] * query_vec * inv_root
    grad_negative = -coef[:, :, None] * query_vec[:, None, :] * inv_root
    states = jnp.concatenate(
        [query_cls, positive_cls, negative_cls.reshape(-1, width)], axis=0
    ).astype(jnp.float32)
    factors = jnp.concatenate([grad_query, grad_positive, grad_negative.reshape(-1, width)], axis=0)
    empty = jnp.zeros((width, width), jnp.float32)
    dense_grad = add_outer(
        empty,
        (
            lax.all_gather(states, ("group", "shard"), axis=0, tiled=True),
            lax.all_gather(factors, ("group", "shard"), axis=0, tiled=True),
        ),
    )
    return (margin, dense_grad)


def solution(mesh):
    in_specs = (
        P(("group", "shard"), None, None),
        P(("group", "shard"), None, None),
        P("shard", None, None),
        P(("group", "shard"), None),
        P(("group", "shard"), None),
        P(),
        P(None, "shard"),
        P(),
    )
    out_specs = (P(("group", "shard"), None), P())
    return jax.shard_map(body, mesh=mesh, in_specs=in_specs, out_specs=out_specs, check_vma=False)
```

profile of v0, /device:TPU:0, one launch (start us, length us, event | category | flops | bytes accessed | tf_op | source)
XLA Modules:
  0.0 263.6 jit_solution(15380211158896153419)
XLA Ops:
  7.2 0.8 and_select_fusion.2
  8.6 9.7 %all_to_all.11 = s32[8,1,2]{2,1,0:T(1,128)S(1)} all-to-all(s32[8,1,2]{2,1,0:T(1,128)S(1)} %copy.29), channel_id=1, replica_groups=mesh['group'=4,'shard'=8] {'shard'}, dimensions={0} | all-to-all | bytes 128 | tf_op jit(solution)/shard_map/all_to_all | solution.py:62
  18.6 1.8 gather_fusion
  20.4 2.7 %broadcast_select_fusion = bf16[8,2,64,768]{3,2,1,0:T(8,128)(2,1)} fusion(bf16[8,2,64,768]{3,2,1,0:T(8,128)(2,1)} %bitcast.160, pred[8,2]{1,0:T(8,128)(4,1)S(1)} %copy.31), kind=kLoop, calls=%fused_computation.37 | loop fusion | flops 786432 | bytes 3145744 | tf_op jit(solution)/shard_map/jit(_where)/select_n | solution.py:65
  23.1 4.4 %all-to-all-start.1 = ((bf16[8,2,64,768]{3,2,1,0:T(8,128)(2,1)}), bf16[8,2,64,768]{3,2,1,0:T(8,128)(2,1)}, u32[]{:S(2)}, u32[]{:S(2)}) async-start(bf16[8,2,64,768]{3,2,1,0:T(8,128)(2,1)} %broadcast_select_fusion), calls=%async_computation.1 | async-start | bytes 3145728 | tf_op jit(solution)/shard_map/all_to_all | solution.py:66
  27.7 2.0 fusion.77
  30.0 18.5 %all-to-all-done.1 = bf16[8,2,64,768]{3,2,1,0:T(8,128)(2,1)} async-done(((bf16[8,2,64,768]{3,2,1,0:T(8,128)(2,1)}), bf16[8,2,64,768]{3,2,1,0:T(8,128)(2,1)}, u32[]{:S(2)}, u32[]{:S(2)}) %all-to-all-start.1) | async-done | bytes 1572896 | tf_op jit(solution)/shard_map/all_to_all | solution.py:66
  48.6 2.9 %gather_fusion.1 = bf16[8,64,768]{2,1,0:T(8,128)(2,1)} fusion(bf16[16,64,768]{2,1,0:T(8,128)(2,1)} %bitcast.14, s32[1024]{0:T(1024)S(1)} %pad_clamp_fusion), kind=kCustom, calls=%fused_computation.1 | custom fusion | bytes 1572896 | tf_op jit(solution)/shard_map/gather | solution.py:67
  51.4 2.8 %fusion.31 = (u8[64,768]{1,0:T(8,128)(4,1)S(1)}, u8[64,768]{1,0:T(8,128)(4,1)S(1)}, u8[64,768]{1,0:T(8,128)(4,1)S(1)}, f32[8,64,768]{2,1,0:T(8,128)S(1)}) fusion(bf16[8,64,768]{2,1,0:T(8,128)(2,1)} %gather_fusion.1, bf16[768,768]{1,0:T(8,128)(2,1)} %param.15), kind=kOutput, calls=%fused_computation.51 | convolution fusion | flops 611696640 | bytes 3686400 | tf_op jit(solution)/shard_map/dot_general | solution.py:12
  54.3 3.8 %fusion.75 = (f32[8,64]{1,0:T(8,128)S(1)}, f32[8,64,768]{2,1,0:T(8,128)S(1)}) fusion(u8[64,768]{1,0:T(8,128)(4,1)S(1)} %get-tuple-element.38, u8[64,768]{1,0:T(8,128)(4,1)S(1)} %get-tuple-element.39, f32[8,64,768]{2,1,0:T(8,128)S(1)} %get-tuple-element.56, u8[64,768]{1,0:T(8,128)(4,1)S(1)} %get-tuple-element.37), kind=kLoop, calls=%fused_computation.154 | loop fusion | flops 28311040 | bytes 3295232 | tf_op jit(solution)/shard_map/reduce_sum | solution.py:14
  58.7 1.0 maximum_bitcast_fusion
  59.8 0.7 dynamic-slice.1
  60.4 1.6 convolution_reduce_fusion.1
  62.0 1.6 fusion.79
  63.5 0.7 multiply_reduce_fusion.3
  64.9 2.1 fusion.78
  67.3 10.4 %all-gather = bf16[256,768]{1,0:T(8,128)(2,1)S(1)} all-gather(bf16[32,768]{1,0:T(8,128)(2,1)S(1)} %multiply_convert_fusion.2), channel_id=2, replica_groups=mesh['group'=4,'shard'=8] {'shard'}, dimensions={0}, use_global_device_ids=true | all-gather | bytes 442368 | tf_op jit(solution)/shard_map/all_gather | solution.py:49
  77.8 1.4 fusion.20
  79.2 0.9 slice.24
  80.1 50.6 %all-gather.2 = f32[32,10,768]{2,1,0:T(8,128)} all-gather(f32[1,10,768]{2,1,0:T(8,128)S(1)} %fusion.62), channel_id=1, replica_groups=mesh['group'=4,'shard'=8] {'group','shard'}, dimensions={0}, use_global_device_ids=true | all-gather | bytes 1013760 | tf_op jit(solution)/shard_map/all_gather | solution.py:112
  130.8 2.5 reshape.544
  133.3 1.5 fusion.80
  134.8 48.1 %while.2 = (s32[]{:T(128)}, f32[9,8,1920]{2,1,0:T(8,128)}, bf16[9,8,64,768]{3,2,1,0:T(8,128)(2,1)}, bf16[768,1920]{1,0:T(8,128)(2,1)}, s32[]{:T(128)}) while((s32[]{:T(128)}, f32[9,8,1920]{2,1,0:T(8,128)}, bf16[9,8,64,768]{3,2,1,0:T(8,128)(2,1)}, bf16[768,1920]{1,0:T(8,128)(2,1)}, s32[]{:T(128)}) %tuple.40), condition=%wide.region_13.14_spmd, body=%wide.region_11.13_spmd.sunk | while | flops 1511900160 | bytes 3919949 | solution.py:25
  134.8 4.7 %log-plus-one_reduce_fusion.2 = f32[8,1920]{1,0:T(8,128)S(1)} fusion(bf16[768,1920]{1,0:T(8,128)(2,1)} %get-tuple-element.102, bf16[9,8,64,768]{3,2,1,0:T(8,128)(2,1)} %get-tuple-element.101, s32[]{:T(128)S(6)} %copy.45), kind=kOutput, calls=%fused_computation.2.clone.1 | convolution fusion | flops 1511900160 | bytes 3796996 | tf_op jit(solution)/shard_map/while/body/eval_jaxpr/vmap()/dot_general | solution.py:20
  140.2 4.7 %log-plus-one_reduce_fusion.2 = f32[8,1920]{1,0:T(8,128)S(1)} fusion(bf16[768,1920]{1,0:T(8,128)(2,1)} %get-tuple-element.102, bf16[9,8,64,768]{3,2,1,0:T(8,128)(2,1)} %get-tuple-element.101, s32[]{:T(128)S(6)} %copy.45), kind=kOutput, calls=%fused_computation.2.clone.1 | convolution fusion | flops 1511900160 | bytes 3796996 | tf_op jit(solution)/shard_map/while/body/eval_jaxpr/vmap()/dot_general | solution.py:20
  144.9 0.6 bitcast_dynamic-update-slice_fusion.2
  145.5 4.7 %log-plus-one_reduce_fusion.2 = f32[8,1920]{1,0:T(8,128)S(1)} fusion(bf16[768,1920]{1,0:T(8,128)(2,1)} %get-tuple-element.102, bf16[9,8,64,768]{3,2,1,0:T(8,128)(2,1)} %get-tuple-element.101, s32[]{:T(128)S(6)} %copy.45), kind=kOutput, calls=%fused_computation.2.clone.1 | convolution fusion | flops 1511900160 | bytes 3796996 | tf_op jit(solution)/shard_map/while/body/eval_jaxpr/vmap()/dot_general | solution.py:20
  150.3 0.6 bitcast_dynamic-update-slice_fusion.2
  150.9 4.7 %log-plus-one_reduce_fusion.2 = f32[8,1920]{1,0:T(8,128)S(1)} fusion(bf16[768,1920]{1,0:T(8,128)(2,1)} %get-tuple-element.102, bf16[9,8,64,768]{3,2,1,0:T(8,128)(2,1)} %get-tuple-element.101, s32[]{:T(128)S(6)} %copy.45), kind=kOutput, calls=%fused_computation.2.clone.1 | convolution fusion | flops 1511900160 | bytes 3796996 | tf_op jit(solution)/shard_map/while/body/eval_jaxpr/vmap()/dot_general | solution.py:20
  155.6 0.6 bitcast_dynamic-update-slice_fusion.2
  156.2 4.7 %log-plus-one_reduce_fusion.2 = f32[8,1920]{1,0:T(8,128)S(1)} fusion(bf16[768,1920]{1,0:T(8,128)(2,1)} %get-tuple-element.102, bf16[9,8,64,768]{3,2,1,0:T(8,128)(2,1)} %get-tuple-element.101, s32[]{:T(128)S(6)} %copy.45), kind=kOutput, calls=%fused_computation.2.clone.1 | convolution fusion | flops 1511900160 | bytes 3796996 | tf_op jit(solution)/shard_map/while/body/eval_jaxpr/vmap()/dot_general | solution.py:20
  160.9 0.6 bitcast_dynamic-update-slice_fusion.2
  161.6 4.7 %log-plus-one_reduce_fusion.2 = f32[8,1920]{1,0:T(8,128)S(1)} fusion(bf16[768,1920]{1,0:T(8,128)(2,1)} %get-tuple-element.102, bf16[9,8,64,768]{3,2,1,0:T(8,128)(2,1)} %get-tuple-element.101, s32[]{:T(128)S(6)} %copy.45), kind=kOutput, calls=%fused_computation.2.clone.1 | convolution fusion | flops 1511900160 | bytes 3796996 | tf_op jit(solution)/shard_map/while/body/eval_jaxpr/vmap()/dot_general | solution.py:20
  166.3 0.6 bitcast_dynamic-update-slice_fusion.2
  166.9 4.7 %log-plus-one_reduce_fusion.2 = f32[8,1920]{1,0:T(8,128)S(1)} fusion(bf16[768,1920]{1,0:T(8,128)(2,1)} %get-tuple-element.102, bf16[9,8,64,768]{3,2,1,0:T(8,128)(2,1)} %get-tuple-element.101, s32[]{:T(128)S(6)} %copy.45), kind=kOutput, calls=%fused_computation.2.clone.1 | convolution fusion | flops 1511900160 | bytes 3796996 | tf_op jit(solution)/shard_map/while/body/eval_jaxpr/vmap()/dot_general | solution.py:20
  171.6 0.6 bitcast_dynamic-update-slice_fusion.2
  172.3 4.7 %log-plus-one_reduce_fusion.2 = f32[8,1920]{1,0:T(8,128)S(1)} fusion(bf16[768,1920]{1,0:T(8,128)(2,1)} %get-tuple-element.102, bf16[9,8,64,768]{3,2,1,0:T(8,128)(2,1)} %get-tuple-element.101, s32[]{:T(128)S(6)} %copy.45), kind=kOutput, calls=%fused_computation.2.clone.1 | convolution fusion | flops 1511900160 | bytes 3796996 | tf_op jit(solution)/shard_map/while/body/eval_jaxpr/vmap()/dot_general | solution.py:20
  177.6 4.7 %log-plus-one_reduce_fusion.2 = f32[8,1920]{1,0:T(8,128)S(1)} fusion(bf16[768,1920]{1,0:T(8,128)(2,1)} %get-tuple-element.102, bf16[9,8,64,768]{3,2,1,0:T(8,128)(2,1)} %get-tuple-element.101, s32[]{:T(128)S(6)} %copy.45), kind=kOutput, calls=%fused_computation.2.clone.1 | convolution fusion | flops 1511900160 | bytes 3796996 | tf_op jit(solution)/shard_map/while/body/eval_jaxpr/vmap()/dot_general | solution.py:20
  182.9 2.1 reshape_reshape.3
  185.0 2.5 fusion.56
  187.5 12.1 %all-reduce = f32[8,9]{1,0:T(8,128)S(1)} all-reduce(f32[8,9]{1,0:T(8,128)S(1)} %bitcast.165), channel_id=4, replica_groups=mesh['group'=4,'shard'=8] {'shard'}, use_global_device_ids=true, to_apply=%region_14.15.clone | all-reduce | flops 72 | bytes 576
  199.6 0.6 dynamic-slice_multiply_fusion
  200.3 1.4 fusion.74
  201.9 0.7 multiply_multiply_fusion.16
  202.6 0.7 subtract_multiply_fusion
  203.4 44.1 %all-gather.3 = f32[32,10,768]{2,1,0:T(8,128)} all-gather(f32[1,10,768]{2,1,0:T(8,128)S(1)} %maximum_bitcast_fusion.1), channel_id=1, replica_groups=mesh['group'=4,'shard'=8] {'group','shard'}, dimensions={0}, use_global_device_ids=true | all-gather | bytes 1013760 | tf_op jit(solution)/shard_map/all_gather | solution.py:113
  247.5 2.4 reshape.546
  249.9 6.9 %fusion.81 = f32[768,768]{1,0:T(8,128)} fusion(f32[320,768]{1,0:T(8,128)} %reshape.544, f32[320,768]{1,0:T(8,128)} %reshape.546), kind=kOutput, calls=%fused_computation.159 | convolution fusion | flops 2264924160 | bytes 4325376 | tf_op jit(solution)/shard_map/rd,re->de/dot_general | solution.py:29
  (60 shorter events, 4.4 us)
Async XLA Ops:
  7.2 11.4 %copy-start = (bf16[32,64,768]{2,1,0:T(8,128)(2,1)S(1)}, bf16[32,64,768]{2,1,0:T(8,128)(2,1)}, u32[]{:S(2)}) copy-start(bf16[32,64,768]{2,1,0:T(8,128)(2,1)} %param.12) | copy-start | bytes 9437188
  23.1 4.5 %copy-start.5 = (s32[1,8]{1,0:T(1,128)S(1)}, s32[1,8]{1,0:T(1,128)}, u32[]{:S(2)}) copy-start(s32[1,8]{1,0:T(1,128)} %param.13) | copy-start | bytes 100
  23.1 4.5 %copy-start.2 = (bf16[1,64,768]{2,1,0:T(8,128)(2,1)S(1)}, bf16[1,64,768]{2,1,0:T(8,128)(2,1)}, u32[]{:S(2)}) copy-start(bf16[1,64,768]{2,1,0:T(8,128)(2,1)} %param.11) | copy-start | bytes 294916
  23.1 25.4 %all-to-all-start.1 = ((bf16[8,2,64,768]{3,2,1,0:T(8,128)(2,1)}), bf16[8,2,64,768]{3,2,1,0:T(8,128)(2,1)}, u32[]{:S(2)}, u32[]{:S(2)}) async-start(bf16[8,2,64,768]{3,2,1,0:T(8,128)(2,1)} %broadcast_select_fusion), calls=%async_computation.1 | async-start | bytes 3145728 | tf_op jit(solution)/shard_map/all_to_all | solution.py:66
  27.6 107.3 %all-gather.6.cloned.1.call-start = ((), (), s32[]{:S(2)}) async-start(), calls=%async_computation.2 | async-start | bytes 7962624 | tf_op jit(solution)/shard_map/all_gather | solution.py:74
  58.7 1.1 copy-start.6
  58.7 3.3 %copy-start.1 = (bf16[1,32,768]{2,1,0:T(8,128)(2,1)S(1)}, bf16[1,32,768]{2,1,0:T(8,128)(2,1)}, u32[]{:S(2)}) copy-start(bf16[1,32,768]{2,1,0:T(8,128)(2,1)} %param.10) | copy-start | bytes 147460
  64.9 12.8 %copy-start.4 = (bf16[768,1920]{1,0:T(8,128)(2,1)S(1)}, bf16[768,1920]{1,0:T(8,128)(2,1)}, u32[]{:S(2)}) copy-start(bf16[768,1920]{1,0:T(8,128)(2,1)} %param.16) | copy-start | bytes 8847364
  182.9 17.4 %copy-start.3 = (s32[1,8]{1,0:T(1,128)S(1)}, s32[1,8]{1,0:T(1,128)}, u32[]{:S(2)}) copy-start(s32[1,8]{1,0:T(1,128)} %param.14) | copy-start | bytes 100
Sparse Core Ops, SparseCore 0:
  59.9 59.8 all-gather.5
where the time goes:
time: 264 us
  blocking collectives  127 us (48%)
  matrix products  66.2 us (25%)
  local copies, waits for them, and re-layouts  19.4 us (7%)
  waiting for transfers between devices  18.6 us (7%)
  between operations  15.1 us (6%)
  other arithmetic  12.9 us (5%)
  starting transfers between devices  4.46 us (2%)
    all_gather x1, blocking collectives, body(): lax.all_gather(states, ('group', 'shard'), axis=0, tiled=True)  50.6 us
    all_gather x1, blocking collectives, body(): lax.all_gather(factors, ('group', 'shard'), axis=0, tiled=True)  44.1 us
    dot_general x10, matrix products, pool_single(): logits = jnp.dot(sequence, vocab_weight, preferred_element_type=jnp.float32)  43.8 us
    all_to_all x1, waiting for transfers between devices, body(): lax.all_to_all(served, 'shard', split_axis=0, concat_axis=0, tiled=True)  18.5 us
    unnamed x1, blocking collectives  12.1 us
    all_gather x1, blocking collectives, body(): lax.all_gather(query_coded, 'shard', axis=0, tiled=True)  10.4 us
    all_to_all x1, blocking collectives, body(): lax.all_to_all(requests, 'shard', split_axis=0, concat_axis=0, tiled=True)  9.68 us
    dot_general x3, matrix products, encode(): jnp.dot(hidden, transform_weight, preferred_element_type=jnp.float32)  6.94 us
  transfers between devices with their start and end apart: 2, of which 1 were waited for; matrix products, arithmetic and copies ran while one was open for 6% of the time, Pallas kernels for 0%

commit v1 on v0

--- a/solution.py
+++ b/solution.py
@@ -6,6 +6,22 @@
 from jax.sharding import PartitionSpec as P
 
 CAP = 2
+
+
+def pairwise_exchange(x, axis, split, join):
+    ways, here = (lax.axis_size(axis), lax.axis_index(axis))
+    width = x.shape[split] // ways
+    shape = list(x.shape)
+    shape[split] = width
+    height = shape[join]
+    shape[join] = height * ways
+    full = jnp.zeros(shape, x.dtype)
+    for mask in range(ways):
+        part = lax.dynamic_slice_in_dim(x, (here ^ mask) * width, width, axis=split)
+        if mask:
+            part = lax.ppermute(part, axis, [(d, d ^ mask) for d in range(ways)])
+        full = lax.dynamic_update_slice_in_dim(full, part, (here ^ mask) * height, axis=join)
+    return full
 
 
 def encode(hidden, transform_weight):
@@ -63,7 +79,7 @@
     is_valid = asked_for >= 0
     served = passage_store[jnp.clip(asked_for, 0, store_rows - 1)]
     served = jnp.where(is_valid[:, :, None, None], served, jnp.zeros((), served.dtype))
-    fetched = lax.all_to_all(served, "shard", split_axis=0, concat_axis=0, tiled=True)
+    fetched = pairwise_exchange(served, "shard", 0, 0)
     negative_hidden = fetched.reshape(shards * CAP, length, width)[owner_of * CAP + slot_rank]
     negative_coded = encode(negative_hidden, transform_weight)
     passages = jnp.concatenate(

time: 264 us -> 265 us (level)
  blocking collectives: 127 us -> 118 us
  local copies, waits for them, and re-layouts: 19.4 us -> 27.6 us
  starting transfers between devices: 4.46 us -> 9.69 us
  waiting for transfers between devices: 18.6 us -> 15.8 us
    all_to_all x1, waiting for transfers between devices: 18.5 us -> 2.08 us  [body(): lax.all_to_all(requests, 'shard', split_axis=0, concat_axis=0, tiled=True)]
    ppermute x0 -> x7, waiting for transfers between devices: none -> 13.7 us  [pairwise_exchange(): part = lax.ppermute(part, axis, [(d, d ^ mask) for d in range(ways)])]
    all_to_all x1 -> x0, blocking collectives: 9.68 us -> none  [body(): lax.all_to_all(requests, 'shard', split_axis=0, concat_axis=0, tiled=True)]
    dynamic_update_slice x0 -> x7, local copies, waits for them, and re-layouts: none -> 4.83 us  [pairwise_exchange(): lax.dynamic_update_slice_in_dim(full, part, (here ^ mask) * height, axis=...]
    ppermute x0 -> x7, starting transfers between devices: none -> 4.46 us  [pairwise_exchange(): part = lax.ppermute(part, axis, [(d, d ^ mask) for d in range(ways)])]
    unnamed x18 -> x16, local copies, waits for them, and re-layouts: 5.61 us -> 5.6 us
  transfers between devices with their start and end apart: 2 -> 9, of which waited for: 1 -> 4; matrix products, arithmetic and copies ran while one was open for 6% -> 8% of each run, Pallas kernels for 0% -> 0%
where the time goes in v1:
time: 265 us; the launch traced here: 264 us
  blocking collectives  118 us (45%)
  matrix products  66.3 us (25%)
  local copies, waits for them, and re-layouts  27.6 us (10%)
  waiting for transfers between devices  15.8 us (6%)
  between operations  15.1 us (6%)
  other arithmetic  11.7 us (4%)
  starting transfers between devices  9.69 us (4%)
    all_gather x1, blocking collectives, body(): lax.all_gather(states, ('group', 'shard'), axis=0, tiled=True)  51.1 us
    all_gather x1, blocking collectives, body(): lax.all_gather(factors, ('group', 'shard'), axis=0, tiled=True)  43.9 us
    dot_general x10, matrix products, pool_single(): logits = jnp.dot(sequence, vocab_weight, preferred_element_type=jnp.float32)  43.8 us
    ppermute x7, waiting for transfers between devices, pairwise_exchange(): part = lax.ppermute(part, axis, [(d, d ^ mask) for d in range(ways)])  13.7 us
    unnamed x1, blocking collectives  12.1 us
    all_gather x1, blocking collectives, body(): lax.all_gather(query_coded, 'shard', axis=0, tiled=True)  10.6 us
    dot_general x3, matrix products, encode(): jnp.dot(hidden, transform_weight, preferred_element_type=jnp.float32)  6.99 us
    dot_general x1, matrix products, add_outer(): jnp.einsum('rd,re->de', pieces[0], pieces[1], precision=lax.Precision.HIG...  6.86 us
  transfers between devices with their start and end apart: 9, of which 4 were waited for; matrix products, arithmetic and copies ran while one was open for 8% of the time, Pallas kernels for 0%

profile of v1, /device:TPU:0, one launch (start us, length us, event | category | flops | bytes accessed | tf_op | source)
XLA Modules:
  0.0 264.0 jit_solution(4247980752473183695)
XLA Ops:
  7.2 0.8 and_select_fusion.2
  9.2 5.2 %all-to-all-start = ((s32[8,1,2]{2,1,0:T(1,128)}), s32[8,1,2]{2,1,0:T(1,128)S(1)}, u32[]{:S(2)}, u32[]{:S(2)}) async-start(s32[8,1,2]{2,1,0:T(1,128)} %copy.29), calls=%async_computation | async-start | bytes 8192 | tf_op jit(solution)/shard_map/all_to_all | solution.py:78
  14.4 2.1 fusion.77
  16.9 2.1 all-to-all-done
  19.3 1.8 gather_fusion
  21.1 1.6 broadcast_select_fusion
  22.7 1.3 broadcast_in_dim.41
  24.0 0.8 constant_dynamic-slice_fusion
  25.5 1.3 collective-permute-start.2
  27.3 1.1 collective-permute-start.4
  28.4 0.9 collective-permute-start.5
  30.0 2.7 %collective-permute-done.1 = bf16[1,2,64,768]{3,2,1,0:T(8,128)(2,1)S(1)} collective-permute-done((bf16[1,2,64,768]{3,2,1,0:T(8,128)(2,1)S(1)}, bf16[1,2,64,768]{3,2,1,0:T(8,128)(2,1)S(1)}, u32[]{:S(2)}, u32[]{:S(2)}) %collective-permute-start.1) | collective-permute-done | bytes 196640 | tf_op jit(solution)/shard_map/ppermute | solution.py:22
  32.7 0.7 constant_dynamic-update-slice_fusion.5
  33.4 2.6 collective-permute-done.2
  37.4 8.5 %collective-permute-done.4 = bf16[1,2,64,768]{3,2,1,0:T(8,128)(2,1)S(1)} collective-permute-done((bf16[1,2,64,768]{3,2,1,0:T(8,128)(2,1)S(1)}, bf16[1,2,64,768]{3,2,1,0:T(8,128)(2,1)S(1)}, u32[]{:S(2)}, u32[]{:S(2)}) %collective-permute-start.4) | collective-permute-done | bytes 196640 | tf_op jit(solution)/shard_map/ppermute | solution.py:22
  47.9 2.9 %gather_fusion.1 = bf16[8,64,768]{2,1,0:T(8,128)(2,1)} fusion(bf16[16,64,768]{2,1,0:T(8,128)(2,1)} %bitcast.14, s32[1024]{0:T(1024)S(1)} %pad_clamp_fusion), kind=kCustom, calls=%fused_computation.1 | custom fusion | bytes 1572896 | tf_op jit(solution)/shard_map/gather | solution.py:83
  50.8 2.8 %fusion.31 = (u8[64,768]{1,0:T(8,128)(4,1)S(1)}, u8[64,768]{1,0:T(8,128)(4,1)S(1)}, u8[64,768]{1,0:T(8,128)(4,1)S(1)}, f32[8,64,768]{2,1,0:T(8,128)S(1)}) fusion(bf16[8,64,768]{2,1,0:T(8,128)(2,1)} %gather_fusion.1, bf16[768,768]{1,0:T(8,128)(2,1)} %param.15), kind=kOutput, calls=%fused_computation.51 | convolution fusion | flops 611696640 | bytes 3686400 | tf_op jit(solution)/shard_map/dot_general | solution.py:28
  53.6 3.8 %fusion.75 = (f32[8,64]{1,0:T(8,128)S(1)}, f32[8,64,768]{2,1,0:T(8,128)S(1)}) fusion(u8[64,768]{1,0:T(8,128)(4,1)S(1)} %get-tuple-element.38, u8[64,768]{1,0:T(8,128)(4,1)S(1)} %get-tuple-element.39, f32[8,64,768]{2,1,0:T(8,128)S(1)} %get-tuple-element.64, u8[64,768]{1,0:T(8,128)(4,1)S(1)} %get-tuple-element.37), kind=kLoop, calls=%fused_computation.169 | loop fusion | flops 28311040 | bytes 3295232 | tf_op jit(solution)/shard_map/reduce_sum | solution.py:30
  58.0 1.0 maximum_bitcast_fusion
  59.7 1.6 convolution_reduce_fusion.1
  61.3 1.6 fusion.79
  64.3 2.1 fusion.78
  66.7 10.6 %all-gather = bf16[256,768]{1,0:T(8,128)(2,1)S(1)} all-gather(bf16[32,768]{1,0:T(8,128)(2,1)S(1)} %multiply_convert_fusion.2), channel_id=2, replica_groups=mesh['group'=4,'shard'=8] {'shard'}, dimensions={0}, use_global_device_ids=true | all-gather | bytes 442368 | tf_op jit(solution)/shard_map/all_gather | solution.py:65
  77.2 0.7 slice_bitcast_fusion
  78.0 1.4 fusion.20
  79.4 0.9 slice.24
  80.3 51.1 %all-gather.2 = f32[32,10,768]{2,1,0:T(8,128)} all-gather(f32[1,10,768]{2,1,0:T(8,128)S(1)} %fusion.62), channel_id=1, replica_groups=mesh['group'=4,'shard'=8] {'group','shard'}, dimensions={0}, use_global_device_ids=true | all-gather | bytes 1013760 | tf_op jit(solution)/shard_map/all_gather | solution.py:128
  131.4 2.5 reshape.544
  133.9 1.5 fusion.80
  135.5 48.1 %while.2 = (s32[]{:T(128)}, f32[9,8,1920]{2,1,0:T(8,128)}, bf16[9,8,64,768]{3,2,1,0:T(8,128)(2,1)}, bf16[768,1920]{1,0:T(8,128)(2,1)}, s32[]{:T(128)}) while((s32[]{:T(128)}, f32[9,8,1920]{2,1,0:T(8,128)}, bf16[9,8,64,768]{3,2,1,0:T(8,128)(2,1)}, bf16[768,1920]{1,0:T(8,128)(2,1)}, s32[]{:T(128)}) %tuple.47), condition=%wide.region_13.14_spmd, body=%wide.region_11.13_spmd.sunk | while | flops 1511900160 | bytes 3919949 | solution.py:41
  135.5 4.7 %log-plus-one_reduce_fusion.2 = f32[8,1920]{1,0:T(8,128)S(1)} fusion(bf16[768,1920]{1,0:T(8,128)(2,1)} %get-tuple-element.110, bf16[9,8,64,768]{3,2,1,0:T(8,128)(2,1)} %get-tuple-element.109, s32[]{:T(128)S(6)} %copy.53), kind=kOutput, calls=%fused_computation.2.clone.1 | convolution fusion | flops 1511900160 | bytes 3796996 | tf_op jit(solution)/shard_map/while/body/eval_jaxpr/vmap()/dot_general | solution.py:36
  140.8 4.7 %log-plus-one_reduce_fusion.2 = f32[8,1920]{1,0:T(8,128)S(1)} fusion(bf16[768,1920]{1,0:T(8,128)(2,1)} %get-tuple-element.110, bf16[9,8,64,768]{3,2,1,0:T(8,128)(2,1)} %get-tuple-element.109, s32[]{:T(128)S(6)} %copy.53), kind=kOutput, calls=%fused_computation.2.clone.1 | convolution fusion | flops 1511900160 | bytes 3796996 | tf_op jit(solution)/shard_map/while/body/eval_jaxpr/vmap()/dot_general | solution.py:36
  146.2 4.7 %log-plus-one_reduce_fusion.2 = f32[8,1920]{1,0:T(8,128)S(1)} fusion(bf16[768,1920]{1,0:T(8,128)(2,1)} %get-tuple-element.110, bf16[9,8,64,768]{3,2,1,0:T(8,128)(2,1)} %get-tuple-element.109, s32[]{:T(128)S(6)} %copy.53), kind=kOutput, calls=%fused_computation.2.clone.1 | convolution fusion | flops 1511900160 | bytes 3796996 | tf_op jit(solution)/shard_map/while/body/eval_jaxpr/vmap()/dot_general | solution.py:36
  151.5 4.7 %log-plus-one_reduce_fusion.2 = f32[8,1920]{1,0:T(8,128)S(1)} fusion(bf16[768,1920]{1,0:T(8,128)(2,1)} %get-tuple-element.110, bf16[9,8,64,768]{3,2,1,0:T(8,128)(2,1)} %get-tuple-element.109, s32[]{:T(128)S(6)} %copy.53), kind=kOutput, calls=%fused_computation.2.clone.1 | convolution fusion | flops 1511900160 | bytes 3796996 | tf_op jit(solution)/shard_map/while/body/eval_jaxpr/vmap()/dot_general | solution.py:36
  156.9 4.7 %log-plus-one_reduce_fusion.2 = f32[8,1920]{1,0:T(8,128)S(1)} fusion(bf16[768,1920]{1,0:T(8,128)(2,1)} %get-tuple-element.110, bf16[9,8,64,768]{3,2,1,0:T(8,128)(2,1)} %get-tuple-element.109, s32[]{:T(128)S(6)} %copy.53), kind=kOutput, calls=%fused_computation.2.clone.1 | convolution fusion | flops 1511900160 | bytes 3796996 | tf_op jit(solution)/shard_map/while/body/eval_jaxpr/vmap()/dot_general | solution.py:36
  162.2 4.7 %log-plus-one_reduce_fusion.2 = f32[8,1920]{1,0:T(8,128)S(1)} fusion(bf16[768,1920]{1,0:T(8,128)(2,1)} %get-tuple-element.110, bf16[9,8,64,768]{3,2,1,0:T(8,128)(2,1)} %get-tuple-element.109, s32[]{:T(128)S(6)} %copy.53), kind=kOutput, calls=%fused_computation.2.clone.1 | convolution fusion | flops 1511900160 | bytes 3796996 | tf_op jit(solution)/shard_map/while/body/eval_jaxpr/vmap()/dot_general | solution.py:36
  167.6 4.7 %log-plus-one_reduce_fusion.2 = f32[8,1920]{1,0:T(8,128)S(1)} fusion(bf16[768,1920]{1,0:T(8,128)(2,1)} %get-tuple-element.110, bf16[9,8,64,768]{3,2,1,0:T(8,128)(2,1)} %get-tuple-element.109, s32[]{:T(128)S(6)} %copy.53), kind=kOutput, calls=%fused_computation.2.clone.1 | convolution fusion | flops 1511900160 | bytes 3796996 | tf_op jit(solution)/shard_map/while/body/eval_jaxpr/vmap()/dot_general | solution.py:36
  172.9 4.7 %log-plus-one_reduce_fusion.2 = f32[8,1920]{1,0:T(8,128)S(1)} fusion(bf16[768,1920]{1,0:T(8,128)(2,1)} %get-tuple-element.110, bf16[9,8,64,768]{3,2,1,0:T(8,128)(2,1)} %get-tuple-element.109, s32[]{:T(128)S(6)} %copy.53), kind=kOutput, calls=%fused_computation.2.clone.1 | convolution fusion | flops 1511900160 | bytes 3796996 | tf_op jit(solution)/shard_map/while/body/eval_jaxpr/vmap()/dot_general | solution.py:36
  178.2 4.7 %log-plus-one_reduce_fusion.2 = f32[8,1920]{1,0:T(8,128)S(1)} fusion(bf16[768,1920]{1,0:T(8,128)(2,1)} %get-tuple-element.110, bf16[9,8,64,768]{3,2,1,0:T(8,128)(2,1)} %get-tuple-element.109, s32[]{:T(128)S(6)} %copy.53), kind=kOutput, calls=%fused_computation.2.clone.1 | convolution fusion | flops 1511900160 | bytes 3796996 | tf_op jit(solution)/shard_map/while/body/eval_jaxpr/vmap()/dot_general | solution.py:36
  183.6 2.1 reshape_reshape.3
  185.7 2.5 fusion.56
  188.1 12.1 %all-reduce = f32[8,9]{1,0:T(8,128)S(1)} all-reduce(f32[8,9]{1,0:T(8,128)S(1)} %bitcast.165), channel_id=4, replica_groups=mesh['group'=4,'shard'=8] {'shard'}, use_global_device_ids=true, to_apply=%region_14.15.clone | all-reduce | flops 72 | bytes 576
  201.0 1.4 fusion.74
  202.6 0.7 multiply_multiply_fusion.16
  203.3 0.7 subtract_multiply_fusion
  204.0 43.9 %all-gather.3 = f32[32,10,768]{2,1,0:T(8,128)} all-gather(f32[1,10,768]{2,1,0:T(8,128)S(1)} %maximum_bitcast_fusion.1), channel_id=1, replica_groups=mesh['group'=4,'shard'=8] {'group','shard'}, dimensions={0}, use_global_device_ids=true | all-gather | bytes 1013760 | tf_op jit(solution)/shard_map/all_gather | solution.py:129
  247.9 2.4 reshape.546
  250.3 6.9 %fusion.81 = f32[768,768]{1,0:T(8,128)} fusion(f32[320,768]{1,0:T(8,128)} %reshape.544, f32[320,768]{1,0:T(8,128)} %reshape.546), kind=kOutput, calls=%fused_computation.174 | convolution fusion | flops 2264924160 | bytes 4325376 | tf_op jit(solution)/shard_map/rd,re->de/dot_general | solution.py:45
  (80 shorter events, 16.1 us)
Async XLA Ops:
  7.2 12.2 %copy-start = (bf16[32,64,768]{2,1,0:T(8,128)(2,1)S(1)}, bf16[32,64,768]{2,1,0:T(8,128)(2,1)}, u32[]{:S(2)}) copy-start(bf16[32,64,768]{2,1,0:T(8,128)(2,1)} %param.12) | copy-start | bytes 9437188
  9.2 9.8 %all-to-all-start = ((s32[8,1,2]{2,1,0:T(1,128)}), s32[8,1,2]{2,1,0:T(1,128)S(1)}, u32[]{:S(2)}, u32[]{:S(2)}) async-start(s32[8,1,2]{2,1,0:T(1,128)} %copy.29), calls=%async_computation | async-start | bytes 8192 | tf_op jit(solution)/shard_map/all_to_all | solution.py:78
  14.4 121.1 %all-gather.6.cloned.1.call-start = ((), (), s32[]{:S(2)}) async-start(), calls=%async_computation.1 | async-start | bytes 7962624 | tf_op jit(solution)/shard_map/all_gather | solution.py:90
  24.0 0.8 copy-start.4
  24.8 3.6 %collective-permute-start = (bf16[1,2,64,768]{3,2,1,0:T(8,128)(2,1)S(1)}, bf16[1,2,64,768]{3,2,1,0:T(8,128)(2,1)S(1)}, u32[]{:S(2)}, u32[]{:S(2)}) collective-permute-start(bf16[1,2,64,768]{3,2,1,0:T(8,128)(2,1)S(1)} %get-tuple-element.58), channel_id=1, source_target_pairs={{0,1},{1,0},{2,3},{3,2},{4,5},{5,4},{6,7},{7,6},{8,9},{9,8},{10,11... | collective-permute-start | bytes 589832 | tf_op jit(solution)/shard_map/ppermute | solution.py:22
  24.8 7.8 %collective-permute-start.1 = (bf16[1,2,64,768]{3,2,1,0:T(8,128)(2,1)S(1)}, bf16[1,2,64,768]{3,2,1,0:T(8,128)(2,1)S(1)}, u32[]{:S(2)}, u32[]{:S(2)}) collective-permute-start(bf16[1,2,64,768]{3,2,1,0:T(8,128)(2,1)S(1)} %get-tuple-element.57), channel_id=1, source_target_pairs={{0,2},{1,3},{2,0},{3,1},{4,6},{5,7},{6,4},{7,5},{8,10},{9,11},{10,... | collective-permute-start | bytes 589832 | tf_op jit(solution)/shard_map/ppermute | solution.py:22
  25.5 10.5 %collective-permute-start.2 = (bf16[1,2,64,768]{3,2,1,0:T(8,128)(2,1)S(1)}, bf16[1,2,64,768]{3,2,1,0:T(8,128)(2,1)S(1)}, u32[]{:S(2)}, u32[]{:S(2)}) collective-permute-start(bf16[1,2,64,768]{3,2,1,0:T(8,128)(2,1)S(1)} %get-tuple-element.56), channel_id=1, source_target_pairs={{0,3},{1,2},{2,1},{3,0},{4,7},{5,6},{6,5},{7,4},{8,11},{9,10},{10,... | collective-permute-start | bytes 589832 | tf_op jit(solution)/shard_map/ppermute | solution.py:22
  26.8 9.9 %collective-permute-start.3 = (bf16[1,2,64,768]{3,2,1,0:T(8,128)(2,1)S(1)}, bf16[1,2,64,768]{3,2,1,0:T(8,128)(2,1)S(1)}, u32[]{:S(2)}, u32[]{:S(2)}) collective-permute-start(bf16[1,2,64,768]{3,2,1,0:T(8,128)(2,1)S(1)} %get-tuple-element.55), channel_id=1, source_target_pairs={{0,4},{1,5},{2,6},{3,7},{4,0},{5,1},{6,2},{7,3},{8,12},{9,13},{10,... | collective-permute-start | bytes 589832 | tf_op jit(solution)/shard_map/ppermute | solution.py:22
  27.3 18.5 %collective-permute-start.4 = (bf16[1,2,64,768]{3,2,1,0:T(8,128)(2,1)S(1)}, bf16[1,2,64,768]{3,2,1,0:T(8,128)(2,1)S(1)}, u32[]{:S(2)}, u32[]{:S(2)}) collective-permute-start(bf16[1,2,64,768]{3,2,1,0:T(8,128)(2,1)S(1)} %get-tuple-element.54), channel_id=1, source_target_pairs={{0,5},{1,4},{2,7},{3,6},{4,1},{5,0},{6,3},{7,2},{8,13},{9,12},{10,... | collective-permute-start | bytes 589832 | tf_op jit(solution)/shard_map/ppermute | solution.py:22
  28.4 18.1 %collective-permute-start.5 = (bf16[1,2,64,768]{3,2,1,0:T(8,128)(2,1)S(1)}, bf16[1,2,64,768]{3,2,1,0:T(8,128)(2,1)S(1)}, u32[]{:S(2)}, u32[]{:S(2)}) collective-permute-start(bf16[1,2,64,768]{3,2,1,0:T(8,128)(2,1)S(1)} %get-tuple-element.53), channel_id=1, source_target_pairs={{0,6},{1,7},{2,4},{3,5},{4,2},{5,3},{6,0},{7,1},{8,14},{9,15},{10,... | collective-permute-start | bytes 589832 | tf_op jit(solution)/shard_map/ppermute | solution.py:22
  32.7 14.5 %collective-permute-start.6 = (bf16[1,2,64,768]{3,2,1,0:T(8,128)(2,1)S(1)}, bf16[1,2,64,768]{3,2,1,0:T(8,128)(2,1)S(1)}, u32[]{:S(2)}, u32[]{:S(2)}) collective-permute-start(bf16[1,2,64,768]{3,2,1,0:T(8,128)(2,1)S(1)} %get-tuple-element.52), channel_id=1, source_target_pairs={{0,7},{1,6},{2,5},{3,4},{4,3},{5,2},{6,1},{7,0},{8,15},{9,14},{10,... | collective-permute-start | bytes 589832 | tf_op jit(solution)/shard_map/ppermute | solution.py:22
  58.0 1.1 copy-start.5
  58.0 3.3 %copy-start.1 = (bf16[1,32,768]{2,1,0:T(8,128)(2,1)S(1)}, bf16[1,32,768]{2,1,0:T(8,128)(2,1)}, u32[]{:S(2)}) copy-start(bf16[1,32,768]{2,1,0:T(8,128)(2,1)} %param.10) | copy-start | bytes 147460
  64.3 13.7 %copy-start.3 = (bf16[768,1920]{1,0:T(8,128)(2,1)S(1)}, bf16[768,1920]{1,0:T(8,128)(2,1)}, u32[]{:S(2)}) copy-start(bf16[768,1920]{1,0:T(8,128)(2,1)} %param.16) | copy-start | bytes 8847364
  183.6 17.4 %copy-start.2 = (s32[1,8]{1,0:T(1,128)S(1)}, s32[1,8]{1,0:T(1,128)}, u32[]{:S(2)}) copy-start(s32[1,8]{1,0:T(1,128)} %param.14) | copy-start | bytes 100
Sparse Core Ops, SparseCore 0:
  59.2 59.3 all-gather.5
